TPU v7x, 32 devices: a whole 2x2x4 slice. The times are simulated.
32 devices in a mesh: row: 8 (over y, x, core), col: 4 (over z).
Axes of the slice: x: 2, y: 2, z: 4, core: 2. Of those that a mesh axis runs over, the one named last changes fastest.
Arguments:
- attn_out: bfloat16 [2, 256, 16384], P(None, 'row', 'col'), may hold values from -6 to 6
- o_weight: bfloat16 [16384, 16384], P('col', 'row'), may hold values from -0.046875 to 0.046875
- residual: float32 [2, 256, 16384], P(None, 'col', 'row'), may hold values from -73 to 73
- norm_gain: float32 [16384], replicated, may hold values from 0.5 to 1.5
- gram_in: float32 [16384, 16384], P('row', 'col'), may hold values from -0.1 to 1.5
Outputs:
- gram: float32 [16384, 16384], P('row', 'col')
All inputs are finite; a program needn't handle non-finite values.
Results may differ from a plain program's by a relative error of at most 0.0003.
Values may be sent and summed in bfloat16 or wider, within the bound.
A program may use at most 192 MiB of HBM per device.

v0:
```python
import jax
import jax.numpy as jnp
from jax import lax
from jax.sharding import PartitionSpec as P

epsilon_norm = 1e-05
highest = lax.Precision.HIGHEST


def spread(block, axis, owner):
    block = jnp.where(lax.axis_index(axis) == owner, block, jnp.zeros_like(block))
    return lax.psum(block, axis)


def outer_sum(left_rows, right_rows):
    return lax.dot_general(
        left_rows,
        right_rows,
        (((0,), (0,)), ((), ())),
        precision=highest,
        preferred_element_type=jnp.float32,
    )


def body(attn_out, o_weight, residual, norm_gain, gram_in):
    row_count = lax.axis_size("row")
    col_count = lax.axis_size("col")
    fan_ratio = row_count // col_count
    row_index = lax.axis_index("row")
    col_index = lax.axis_index("col")
    col_width = o_weight.shape[0]
    row_width = o_weight.shape[1]
    model_width = row_width * row_count
    group_tokens = attn_out.shape[1] * row_count
    local_tokens = residual.shape[1]
    gain_rows = lax.dynamic_slice_in_dim(norm_gain, row_index * row_width, row_width)
    gram_sum = jnp.zeros((row_width, col_width), jnp.float32)
    for block_index in range(attn_out.shape[0]):
        resid_block = residual[block_index]
        partial_value = jnp.dot(
            lax.all_gather(attn_out[block_index], "row", axis=0, tiled=True),
            o_weight,
            preferred_element_type=jnp.float32,
        )
        offset = col_index * local_tokens
        own_rows = lax.dynamic_slice_in_dim(partial_value, offset, local_tokens, 0) + resid_block
        partial_value = lax.dynamic_update_slice_in_dim(partial_value, own_rows, offset, 0)
        row_panel = lax.psum(partial_value, "col")
        panel_sums = lax.psum(jnp.sum(row_panel * row_panel, axis=1), "row")
        inverse_rms = lax.rsqrt(panel_sums / model_width + epsilon_norm)
        row_panel = row_panel * inverse_rms[:, None] * gain_rows[None, :]
        column_parts = []
        for member in range(fan_ratio):
            column_parts.append(spread(row_panel, "row", col_index * fan_ratio + member))
        column_block = jnp.concatenate(column_parts, axis=1)
        gram_sum = gram_sum + outer_sum(row_panel, column_block)
    return gram_in + gram_sum / (attn_out.shape[0] * group_tokens)


def solution(mesh):
    return jax.shard_map(
        body,
        mesh=mesh,
        in_specs=(
            P(None, "row", "col"),
            P("col", "row"),
            P(None, "col", "row"),
            P(),
            P("row", "col"),
        ),
        out_specs=P("row", "col"),
        check_vma=False,
    )
```

profile of v0, /device:TPU:0, one launch (start us, length us, event | category | flops | bytes accessed | tf_op | source)
XLA Modules:
  0.0 466.1 jit_solution(1088472988798540097)
XLA Ops:
  6.5 1.8 fusion.23
  8.4 0.0 all-gather.7.cloned.1.call-update
  8.4 0.0 all-gather.5.cloned.1.call-start
  8.5 0.7 all-gather.5.cloned.1.call-update
  9.2 0.0 all-reduce.8.cloned.1.call-start
  9.2 30.5 %all-gather.7.cloned.1.call-done = bf16[1,256,4096]{2,1,0:T(8,128)(2,1)} async-done(((bf16[1,32,4096]{2,1,0:T(8,128)(2,1)}), bf16[1,256,4096]{2,1,0:T(8,128)(2,1)}) %all-gather.7.cloned.1.call-update) | async-done | bytes 2097168 | tf_op jit(solution)/shard_map/all_gather | solution.py:41
  39.8 8.7 %fusion.7 = f32[256,2048]{1,0:T(8,128)S(1)} fusion(bf16[4096,2048]{1,0:T(8,128)(2,1)} %param.6, bf16[1,256,4096]{2,1,0:T(8,128)(2,1)} %all-gather.7.cloned.1.call-done), kind=kOutput, calls=%fused_computation.8 | convolution fusion | flops 4294967296 | bytes 20971520 | tf_op jit(solution)/shard_map/dot_general | solution.py:40
  48.5 0.0 copy-start.3
  48.5 21.0 %all-gather.5.cloned.1.call-done = bf16[1,256,4096]{2,1,0:T(8,128)(2,1)} async-done(((bf16[1,32,4096]{2,1,0:T(8,128)(2,1)}), bf16[1,256,4096]{2,1,0:T(8,128)(2,1)}) %all-gather.5.cloned.1.call-update) | async-done | bytes 2097168 | tf_op jit(solution)/shard_map/all_gather | solution.py:41
  69.5 8.7 %fusion.9 = f32[256,2048]{1,0:T(8,128)S(1)} fusion(bf16[4096,2048]{1,0:T(8,128)(2,1)} %param.6, bf16[1,256,4096]{2,1,0:T(8,128)(2,1)} %all-gather.5.cloned.1.call-done), kind=kOutput, calls=%fused_computation.10 | convolution fusion | flops 4294967296 | bytes 20971520 | tf_op jit(solution)/shard_map/dot_general | solution.py:40
  78.2 0.2 fusion.19
  78.4 1.3 copy-done.2
  79.7 1.3 copy-done.1
  81.1 0.0 all-reduce.8.cloned.1.call-update
  81.1 0.0 all-reduce.6.cloned.1.call-start
  81.2 0.7 dynamic_slice.10
  81.9 154.4 %all-reduce.8.cloned.1.call-done = (f32[256,2048]{1,0:T(8,128)}, f32[256,2048]{1,0:T(8,128)}) async-done(((f32[256,2048]{1,0:T(8,128)}, f32[256,2048]{1,0:T(8,128)}), (f32[256,2048]{1,0:T(8,128)}, f32[256,2048]{1,0:T(8,128)})) %all-reduce.8.cloned.1.call-update) | async-done | bytes 4194320 | tf_op jit(solution)/shard_map/psum | solution.py:48
  236.3 2.7 multiply_reduce_fusion
  239.0 13.6 %all-reduce = (f32[256]{0:T(256)S(1)}, f32[256]{0:T(256)S(1)}) all-reduce(f32[256]{0:T(256)S(1)} %get-tuple-element.24, f32[256]{0:T(256)S(1)} %get-tuple-element.23), channel_id=1, replica_groups=mesh['row'=8,'col'=4] {'row'}, use_global_device_ids=true, to_apply=%region_2.0 | all-reduce | flops 512 | bytes 4096 | tf_op jit(solution)/shard_map/psum | solution.py:49
  252.6 5.4 %fusion.14 = (f32[256,2048]{1,0:T(8,128)}, f32[256,2048]{1,0:T(8,128)}, f32[256,2048]{1,0:T(8,128)}, f32[256,2048]{1,0:T(8,128)}) fusion(f32[256,2048]{1,0:T(8,128)} %get-tuple-element.12, f32[256]{0:T(256)S(1)} %add_rsqrt_fusion, f32[2048]{0:T(1024)S(1)} %dynamic_slice.10, pred[]{:T(512)S(6)} %eq.8, pred[]{:T(512)S(6)} %eq.9, f32[256,2048]{1,0:T(8,128)S(1)} %copy-done, ...), kind=kLoop, calls=%fused_computation.19 | loop fusion | flops 4194304 | bytes 12593154 | tf_op jit(solution)/shard_map/jit(_where)/select_n | solution.py:11
  258.1 0.0 all-reduce.6.cloned.1.call-update
  258.1 123.8 %all-reduce.6.cloned.1.call-done = (f32[256,2048]{1,0:T(8,128)}, f32[256,2048]{1,0:T(8,128)}, f32[256,2048]{1,0:T(8,128)}, f32[256,2048]{1,0:T(8,128)}) async-done(((f32[256,2048]{1,0:T(8,128)}, f32[256,2048]{1,0:T(8,128)}, f32[256,2048]{1,0:T(8,128)}, f32[256,2048]{1,0:T(8,128)}), (f32[256,2048]{1,0:T(8,128)}, f32[256,2048]{1,0:T(8,128)}, f32[256,2048]{1,0:T(8,128)}, ...) | async-done | bytes 8388624 | tf_op jit(solution)/shard_map/psum | solution.py:12
  381.8 32.2 %fusion = f32[2048,4096]{1,0:T(8,128)} fusion(f32[256,2048]{1,0:T(8,128)} %get-tuple-element.7, f32[256,2048]{1,0:T(8,128)} %get-tuple-element.8, f32[256,2048]{1,0:T(8,128)S(1)} %copy-done, f32[2048]{0:T(1024)S(1)} %dynamic_slice.10, f32[256]{0:T(256)S(1)} %add_rsqrt_fusion.1), kind=kOutput, calls=%fused_computation.1 | convolution fusion | flops 25771900928 | bytes 39855104 | tf_op jit(solution)/shard_map/dot_general | solution.py:16
  414.0 45.6 %multiply_add_fusion = f32[2048,4096]{1,0:T(8,128)} fusion(f32[2048,4096]{1,0:T(8,128)} %param.9, f32[2048,4096]{1,0:T(8,128)} %fusion, f32[256,2048]{1,0:T(8,128)} %get-tuple-element.9, f32[256,2048]{1,0:T(8,128)} %get-tuple-element.10, f32[256,2048]{1,0:T(8,128)} %get-tuple-element.12, f32[256]{0:T(256)S(1)} %add_rsqrt_fusion, f32[2048]{0:T(1024)S(1)} %dynamic_slice.10), kind=kOutput, calls=%fused_computation | convolution fusion | flops 25797066752 | bytes 106963968 | tf_op jit(solution)/shard_map/dot_general | solution.py:16
  (8 shorter events, 0.0 us)
Async XLA Ops:
  6.5 33.2 %all-gather.7.cloned.1.call-start = ((), (), s32[]{:S(2)}) async-start(), calls=%async_computation.1 | async-start | bytes 2359296 | tf_op jit(solution)/shard_map/all_gather | solution.py:41
  8.4 61.1 %all-gather.5.cloned.1.call-start = ((), (), s32[]{:S(2)}) async-start(), calls=%async_computation | async-start | bytes 2359296 | tf_op jit(solution)/shard_map/all_gather | solution.py:41
  9.2 227.1 %all-reduce.8.cloned.1.call-start = ((), (), s32[]{:S(2)}) async-start(), calls=%async_computation.3 | async-start | bytes 8388608 | tf_op jit(solution)/shard_map/psum | solution.py:48
  48.5 29.7 %copy-start.3 = (f32[2,64,2048]{2,1,0:T(8,128)S(1)}, f32[2,64,2048]{2,1,0:T(8,128)}, u32[]{:S(2)}) copy-start(f32[2,64,2048]{2,1,0:T(8,128)} %param.7) | copy-start | bytes 3145732
  78.4 1.3 copy-start.2
  79.7 1.3 copy-start.1
  81.1 300.7 %all-reduce.6.cloned.1.call-start = ((), (), s32[]{:S(2)}) async-start(), calls=%async_computation.2 | async-start | bytes 16777216 | tf_op jit(solution)/shard_map/psum | solution.py:12
  236.3 16.4 %copy-start = (f32[256,2048]{1,0:T(8,128)S(1)}, f32[256,2048]{1,0:T(8,128)}, u32[]{:S(2)}) copy-start(f32[256,2048]{1,0:T(8,128)} %get-tuple-element.11) | copy-start | bytes 6291460
Sparse Core Ops, SparseCore 0:
  9.2 30.4 all-gather.6
  41.6 27.7 all-gather.4
  81.2 155.0 all-reduce.7
  258.2 123.5 all-reduce.5
where the time goes:
time: 466 us
  waiting for transfers between devices  330 us (71%)
  matrix products  95.2 us (20%)
  blocking collectives  13.6 us (3%)
  between operations  13.2 us (3%)
  other arithmetic  8.37 us (2%)
  local copies, waits for them, and re-layouts  5.2 us (1%)
    psum x1, waiting for transfers between devices, body(): row_panel = lax.psum(partial_value, 'col')  154 us
    psum x1, waiting for transfers between devices, spread(): return lax.psum(block, axis)  124 us
    dot_general x2, matrix products, outer_sum(): lax.dot_general(left_rows, right_rows, (((0,), (0,)), ((), ())), precisio...  77.8 us
    all_gather x2, waiting for transfers between devices, body(): lax.all_gather(attn_out[block_index], 'row', axis=0, tiled=True)  51.5 us
    dot_general x2, matrix products, body(): jnp.dot(lax.all_gather(attn_out[block_index], 'row', axis=0, tiled=True),...  17.4 us
    psum x1, blocking collectives, body(): panel_sums = lax.psum(jnp.sum(row_panel * row_panel, axis=1), 'row')  13.6 us
  transfers between devices with their start and end apart: 4, of which 4 were waited for; matrix products, arithmetic and copies ran while one was open for 2% of the time, Pallas kernels for 0%

commit v1 on v0

--- a/solution.py
+++ b/solution.py
@@ -45,7 +45,11 @@
         offset = col_index * local_tokens
         own_rows = lax.dynamic_slice_in_dim(partial_value, offset, local_tokens, 0) + resid_block
         partial_value = lax.dynamic_update_slice_in_dim(partial_value, own_rows, offset, 0)
-        row_panel = lax.psum(partial_value, "col")
+        row_panel = partial_value
+        for hop in (1, 2):
+            row_panel = row_panel + lax.ppermute(
+                row_panel, "col", [(dev, dev ^ hop) for dev in range(4)]
+            )
         panel_sums = lax.psum(jnp.sum(row_panel * row_panel, axis=1), "row")
         inverse_rms = lax.rsqrt(panel_sums / model_width + epsilon_norm)
         row_panel = row_panel * inverse_rms[:, None] * gain_rows[None, :]

time: 466 us -> 542 us (1.16)
  waiting for transfers between devices: 330 us -> 399 us
  other arithmetic: 8.37 us -> 14.8 us
    ppermute x0 -> x4, waiting for transfers between devices: none -> 221 us  [body(): lax.ppermute(row_panel, 'col', [(dev, dev ^ hop) for dev in range(4)])]
    psum x1 -> x0, waiting for transfers between devices: 154 us -> none  [body(): row_panel = lax.psum(partial_value, 'col')]
  transfers between devices with their start and end apart: 4 -> 7, of which waited for: 4 -> 7; matrix products, arithmetic and copies ran while one was open for 2% -> 3% of each run, Pallas kernels for 0% -> 0%
where the time goes in v1:
time: 542 us
  waiting for transfers between devices  399 us (74%)
  matrix products  95.2 us (18%)
  other arithmetic  14.8 us (3%)
  between operations  13.2 us (2%)
  blocking collectives  12 us (2%)
    ppermute x4, waiting for transfers between devices, body(): lax.ppermute(row_panel, 'col', [(dev, dev ^ hop) for dev in range(4)])  221 us
    psum x1, waiting for transfers between devices, spread(): return lax.psum(block, axis)  126 us
    dot_general x2, matrix products, outer_sum(): lax.dot_general(left_rows, right_rows, (((0,), (0,)), ((), ())), precisio...  77.8 us
    all_gather x2, waiting for transfers between devices, body(): lax.all_gather(attn_out[block_index], 'row', axis=0, tiled=True)  51.5 us
    dot_general x2, matrix products, body(): jnp.dot(lax.all_gather(attn_out[block_index], 'row', axis=0, tiled=True),...  17.4 us
    psum x1, blocking collectives, body(): panel_sums = lax.psum(jnp.sum(row_panel * row_panel, axis=1), 'row')  12 us
  transfers between devices with their start and end apart: 7, of which 7 were waited for; matrix products, arithmetic and copies ran while one was open for 3% of the time, Pallas kernels for 0%

profile of v1, /device:TPU:0, one launch (start us, length us, event | category | flops | bytes accessed | tf_op | source)
XLA Modules:
  0.0 541.6 jit_solution(1753046472106324020)
XLA Ops:
  6.5 1.8 fusion.23
  8.5 0.7 all-gather.7.cloned.1.call-update
  9.2 30.5 %all-gather.5.cloned.1.call-done = bf16[1,256,4096]{2,1,0:T(8,128)(2,1)} async-done(((bf16[1,32,4096]{2,1,0:T(8,128)(2,1)}), bf16[1,256,4096]{2,1,0:T(8,128)(2,1)}) %all-gather.5.cloned.1.call-update) | async-done | bytes 2097168 | tf_op jit(solution)/shard_map/all_gather | solution.py:41
  39.8 8.7 %fusion.9 = f32[256,2048]{1,0:T(8,128)S(1)} fusion(bf16[4096,2048]{1,0:T(8,128)(2,1)} %param.6, bf16[1,256,4096]{2,1,0:T(8,128)(2,1)} %all-gather.5.cloned.1.call-done), kind=kOutput, calls=%fused_computation.10 | convolution fusion | flops 4294967296 | bytes 20971520 | tf_op jit(solution)/shard_map/dot_general | solution.py:40
  48.5 21.0 %all-gather.7.cloned.1.call-done = bf16[1,256,4096]{2,1,0:T(8,128)(2,1)} async-done(((bf16[1,32,4096]{2,1,0:T(8,128)(2,1)}), bf16[1,256,4096]{2,1,0:T(8,128)(2,1)}) %all-gather.7.cloned.1.call-update) | async-done | bytes 2097168 | tf_op jit(solution)/shard_map/all_gather | solution.py:41
  69.5 8.7 %fusion.7 = f32[256,2048]{1,0:T(8,128)S(1)} fusion(bf16[4096,2048]{1,0:T(8,128)(2,1)} %param.6, bf16[1,256,4096]{2,1,0:T(8,128)(2,1)} %all-gather.7.cloned.1.call-done), kind=kOutput, calls=%fused_computation.8 | convolution fusion | flops 4294967296 | bytes 20971520 | tf_op jit(solution)/shard_map/dot_general | solution.py:40
  78.2 0.2 fusion.20
  78.4 1.6 collective-permute-start
  80.0 0.5 collective-permute-start.2
  80.5 46.5 %collective-permute-done = f32[256,2048]{1,0:T(8,128)S(1)} collective-permute-done((f32[256,2048]{1,0:T(8,128)S(1)}, f32[256,2048]{1,0:T(8,128)S(1)}, u32[]{:S(2)}, u32[]{:S(2)}) %collective-permute-start) | collective-permute-done | bytes 2097184 | tf_op jit(solution)/shard_map/ppermute | solution.py:50
  127.0 1.9 add.57
  128.9 2.5 collective-permute-start.1
  131.4 81.9 %collective-permute-done.2 = f32[256,2048]{1,0:T(8,128)S(1)} collective-permute-done((f32[256,2048]{1,0:T(8,128)S(1)}, f32[256,2048]{1,0:T(8,128)S(1)}, u32[]{:S(2)}, u32[]{:S(2)}) %collective-permute-start.2) | collective-permute-done | bytes 2097184 | tf_op jit(solution)/shard_map/ppermute | solution.py:50
  213.2 1.7 add.63
  214.9 0.7 dynamic_slice.10
  215.6 52.8 %collective-permute-done.1 = f32[256,2048]{1,0:T(8,128)} collective-permute-done((f32[256,2048]{1,0:T(8,128)S(1)}, f32[256,2048]{1,0:T(8,128)}, u32[]{:S(2)}, u32[]{:S(2)}) %collective-permute-start.1) | collective-permute-done | bytes 2097184 | tf_op jit(solution)/shard_map/ppermute | solution.py:50
  268.3 3.1 multiply_reduce_fusion.1
  271.5 39.5 %collective-permute-done.3 = f32[256,2048]{1,0:T(8,128)} collective-permute-done((f32[256,2048]{1,0:T(8,128)}, f32[256,2048]{1,0:T(8,128)}, u32[]{:S(2)}, u32[]{:S(2)}) %collective-permute-start.3) | collective-permute-done | bytes 2097184 | tf_op jit(solution)/shard_map/ppermute | solution.py:50
  311.0 2.5 multiply_reduce_fusion
  313.5 12.0 %all-reduce = (f32[256]{0:T(256)S(1)}, f32[256]{0:T(256)S(1)}) all-reduce(f32[256]{0:T(256)S(1)} %get-tuple-element.13, f32[256]{0:T(256)S(1)} %get-tuple-element.11), channel_id=1, replica_groups=mesh['row'=8,'col'=4] {'row'}, use_global_device_ids=true, to_apply=%region_5.6 | all-reduce | flops 512 | bytes 4096 | tf_op jit(solution)/shard_map/psum | solution.py:53
  325.6 5.4 fusion.12
  331.0 126.3 %all-reduce.4.cloned.1.call-done = (f32[256,2048]{1,0:T(8,128)}, f32[256,2048]{1,0:T(8,128)}, f32[256,2048]{1,0:T(8,128)}, f32[256,2048]{1,0:T(8,128)}) async-done(((f32[256,2048]{1,0:T(8,128)}, f32[256,2048]{1,0:T(8,128)}, f32[256,2048]{1,0:T(8,128)}, f32[256,2048]{1,0:T(8,128)}), (f32[256,2048]{1,0:T(8,128)}, f32[256,2048]{1,0:T(8,128)}, f32[256,2048]{1,0:T(8,128)}, ...) | async-done | bytes 8388624 | tf_op jit(solution)/shard_map/psum | solution.py:12
  457.3 32.2 %fusion.3 = f32[2048,4096]{1,0:T(8,128)} fusion(f32[256,2048]{1,0:T(8,128)} %get-tuple-element.7, f32[256,2048]{1,0:T(8,128)} %get-tuple-element.8, f32[256,2048]{1,0:T(8,128)S(1)} %get-tuple-element.14, f32[256]{0:T(256)S(1)} %get-tuple-element.25, f32[2048]{0:T(1024)S(1)} %dynamic_slice.10), kind=kOutput, calls=%fused_computation.4 | convolution fusion | flops 25771900928 | bytes 39855104 | tf_op jit(solution)/shard_map/dot_general | solution.py:16
  489.5 45.6 %multiply_add_fusion = f32[2048,4096]{1,0:T(8,128)} fusion(f32[2048,4096]{1,0:T(8,128)} %param.9, f32[2048,4096]{1,0:T(8,128)} %fusion.3, f32[256,2048]{1,0:T(8,128)} %get-tuple-element.9, f32[256,2048]{1,0:T(8,128)} %get-tuple-element.10, f32[256,2048]{1,0:T(8,128)} %get-tuple-element.12, f32[2048]{0:T(1024)S(1)} %dynamic_slice.10, f32[256]{0:T(256)S(1)} %get-tuple-element.26), kind=kOutput, calls=%fused_computation | convolution fusion | flops 25797066752 | bytes 106963968 | tf_op jit(solution)/shard_map/dot_general | solution.py:16
  (11 shorter events, 0.1 us)
Async XLA Ops:
  6.5 33.2 %all-gather.5.cloned.1.call-start = ((), (), s32[]{:S(2)}) async-start(), calls=%async_computation | async-start | bytes 2359296 | tf_op jit(solution)/shard_map/all_gather | solution.py:41
  8.4 61.1 %all-gather.7.cloned.1.call-start = ((), (), s32[]{:S(2)}) async-start(), calls=%async_computation.1 | async-start | bytes 2359296 | tf_op jit(solution)/shard_map/all_gather | solution.py:41
  9.2 448.1 %all-reduce.4.cloned.1.call-start = ((), (), s32[]{:S(2)}) async-start(), calls=%async_computation.2 | async-start | bytes 16777216 | tf_op jit(solution)/shard_map/psum | solution.py:12
  48.5 29.7 %copy-start.1 = (f32[2,64,2048]{2,1,0:T(8,128)S(1)}, f32[2,64,2048]{2,1,0:T(8,128)}, u32[]{:S(2)}) copy-start(f32[2,64,2048]{2,1,0:T(8,128)} %param.7) | copy-start | bytes 3145732
  78.4 2.1 copy-start
  78.4 48.6 %collective-permute-start = (f32[256,2048]{1,0:T(8,128)S(1)}, f32[256,2048]{1,0:T(8,128)S(1)}, u32[]{:S(2)}, u32[]{:S(2)}) collective-permute-start(f32[256,2048]{1,0:T(8,128)S(1)} %get-tuple-element.19), channel_id=1, source_target_pairs={{0,1},{1,0},{2,3},{3,2},{4,5},{5,4},{6,7},{7,6},{8,9},{9,8},{10,11... | collective-permute-start | bytes 6291464 | tf_op jit(solution)/shard_map/ppermute | solution.py:50
  80.0 133.2 %collective-permute-start.2 = (f32[256,2048]{1,0:T(8,128)S(1)}, f32[256,2048]{1,0:T(8,128)S(1)}, u32[]{:S(2)}, u32[]{:S(2)}) collective-permute-start(f32[256,2048]{1,0:T(8,128)S(1)} %get-tuple-element.20), channel_id=1, source_target_pairs={{0,1},{1,0},{2,3},{3,2},{4,5},{5,4},{6,7},{7,6},{8,9},{9,8},{10,11... | collective-permute-start | bytes 6291464 | tf_op jit(solution)/shard_map/ppermute | solution.py:50
  128.9 139.5 %collective-permute-start.1 = (f32[256,2048]{1,0:T(8,128)S(1)}, f32[256,2048]{1,0:T(8,128)}, u32[]{:S(2)}, u32[]{:S(2)}) collective-permute-start(f32[256,2048]{1,0:T(8,128)S(1)} %add.57), channel_id=1, source_target_pairs={{0,2},{1,3},{2,0},{3,1},{4,6},{5,7},{6,4},{7,5},{8,10},{9,11},{10,... | collective-permute-start | bytes 6291464 | tf_op jit(solution)/shard_map/ppermute | solution.py:50
  214.9 96.1 %collective-permute-start.3 = (f32[256,2048]{1,0:T(8,128)}, f32[256,2048]{1,0:T(8,128)}, u32[]{:S(2)}, u32[]{:S(2)}) collective-permute-start(f32[256,2048]{1,0:T(8,128)} %add.63), channel_id=1, source_target_pairs={{0,2},{1,3},{2,0},{3,1},{4,6},{5,7},{6,4},{7,5},{8,10},{9,11},{10,... | collective-permute-start | bytes 6291464 | tf_op jit(solution)/shard_map/ppermute | solution.py:50
Sparse Core Ops, SparseCore 0:
  9.2 30.4 all-gather.4
  41.6 27.7 all-gather.6
  331.1 126.1 all-reduce.3
